TPU v7x, 32 devices: a whole 2x2x4 slice. The times are simulated.
32 devices in a mesh: fsdp: 4 (over y, x), grp: 8 (over z, core).
Axes of the slice: x: 2, y: 2, z: 4, core: 2. Of those that a mesh axis runs over, the one named last changes fastest.
Arguments:
- grad_out: bfloat16 [32, 512, 512], P(('fsdp', 'grp')), may hold values from -6 to 6
- pre_first: bfloat16 [32, 512, 512], P(('fsdp', 'grp')), may hold values from -8 to 8
- pre_second: bfloat16 [32, 512, 512], P(('fsdp', 'grp')), may hold values from -8 to 8
- conv_first: bfloat16 [3, 512, 512], P(None, 'fsdp'), may hold values from -0.15625 to 0.15625
- conv_second: bfloat16 [3, 512, 512], P(None, 'fsdp'), may hold values from -0.15625 to 0.15625
- lengths: int32 [32], P(('fsdp', 'grp')), may hold values from 64 to 512
- item_ids: int32 [16384], P('grp'), may hold values from 0 to 8191
- owners: int32 [512, 1], P('grp'), may hold values from 0 to 7; in each aligned block of 64 rows (0 to 63, 64 to 127, ...) at most 16 rows name the same one
Outputs:
- table_grad: float32 [512, 65536], P('fsdp', 'grp')
Inputs may be any that keep to these rules, and one draw needn't show every extreme that they name: `owners`: among the blocks of one group, no owner is named by more than 16 blocks, a bound that some block reaches.
All inputs are finite; a program needn't handle non-finite values.
Results may differ from a plain program's by a relative error of at most 0.0037.
Values may be sent and summed in bfloat16 or wider, within the bound.
A program may use at most 64 MiB of HBM per device.

v0:
```python
import jax
import jax.numpy as jnp
from jax import lax
from jax.sharding import PartitionSpec as P

BLK = 32
ROWS_OWN = 8192


def layer_back(gradient, pre_acts, live_rows, dilation, product):
    seq_len = gradient.shape[0]
    pre_float = pre_acts.astype(jnp.float32)
    sig_val = jax.nn.sigmoid(pre_float)
    deltas = (gradient * sig_val * (1.0 + pre_float * (1.0 - sig_val))).astype(jnp.bfloat16)
    padded = jnp.pad(deltas, ((dilation, dilation), (0, 0)))
    tap_rows = jnp.stack(
        [
            padded[2 * dilation : 2 * dilation + seq_len],
            padded[dilation : dilation + seq_len],
            padded[0:seq_len],
        ]
    )
    return gradient + live_rows * product(tap_rows)


def gathered_product(weights):

    def apply_taps(tap_rows):
        return jnp.einsum(
            "ktd,kpd->tp",
            tap_rows,
            lax.all_gather(weights, "fsdp", axis=1, tiled=True),
            preferred_element_type=jnp.float32,
        )

    return apply_taps


def body(grad_out, pre_first, pre_second, conv_first, conv_second, lengths, item_ids, owners):
    seq_len = grad_out.shape[1]
    positions = jnp.arange(seq_len, dtype=jnp.int32)
    live_rows = (positions < lengths[0]).astype(jnp.float32)[:, None]
    gradient = grad_out[0].astype(jnp.float32)
    gradient = layer_back(gradient, pre_second[0], live_rows, 2, gathered_product(conv_second))
    gradient = layer_back(gradient, pre_first[0], live_rows, 1, gathered_product(conv_first))
    row_grad = (live_rows * gradient).astype(jnp.bfloat16)
    group_cols = lax.all_to_all(row_grad.T, "fsdp", split_axis=0, concat_axis=1, tiled=True)
    feat_cols = group_cols.shape[0]
    owner_count = lax.axis_size("grp")
    blocks = owners.shape[0]
    slot_cap = max(2, 2 * blocks // owner_count)
    block_dest = owners[:, 0]
    dest_hits = (block_dest[:, None] == jnp.arange(owner_count, dtype=jnp.int32)[None, :]).astype(
        jnp.int32
    )
    earlier = jnp.cumsum(dest_hits, axis=0) - dest_hits
    block_rank = jnp.sum(dest_hits * earlier, axis=1)
    slot_index = block_dest * slot_cap + block_rank
    select_int = (
        slot_index[:, None] == jnp.arange(owner_count * slot_cap, dtype=jnp.int32)[None, :]
    ).astype(jnp.int32)
    select_int = select_int.reshape(blocks, owner_count, slot_cap)
    select_map = select_int.astype(jnp.bfloat16)
    block_cols = group_cols.reshape(feat_cols, blocks, BLK)
    send_rows = jnp.einsum(
        "cbr,bos->ocsr", block_cols, select_map, preferred_element_type=jnp.float32
    )
    send_rows = send_rows.astype(jnp.bfloat16).reshape(owner_count, feat_cols, slot_cap * BLK)
    shifted_ids = item_ids.reshape(blocks, BLK) + 1
    send_ids = jnp.einsum("br,bos->osr", shifted_ids, select_int) - 1
    send_ids = send_ids.reshape(owner_count, slot_cap * BLK)
    recv_rows, recv_ids = (
        lax.all_to_all(send_rows, "grp", split_axis=0, concat_axis=0, tiled=True),
        lax.all_to_all(send_ids, "grp", split_axis=0, concat_axis=0, tiled=True),
    )
    flat_rows = jnp.transpose(recv_rows, (0, 2, 1)).reshape(-1, feat_cols).astype(jnp.float32)
    safe_ids = jnp.where(recv_ids < 0, ROWS_OWN, recv_ids).reshape(-1)
    summed = jax.ops.segment_sum(flat_rows, safe_ids, num_segments=ROWS_OWN + 1)
    return summed[:ROWS_OWN].T


def solution(mesh):
    placed = (
        P(("fsdp", "grp"), None, None),
        P(("fsdp", "grp"), None, None),
        P(("fsdp", "grp"), None, None),
        P(None, "fsdp", None),
        P(None, "fsdp", None),
        P(("fsdp", "grp")),
        P("grp"),
        P("grp", None),
    )
    return jax.shard_map(
        body, mesh=mesh, in_specs=placed, out_specs=P("fsdp", "grp"), check_vma=False
    )
```

profile of v0, /device:TPU:0, one launch (start us, length us, event | category | flops | bytes accessed | tf_op | source)
XLA Modules:
  0.0 175.9 jit_solution(7663716986740653124)
XLA Ops:
  6.5 0.7 all-gather.3.cloned.1.call-update
  7.3 0.7 all-gather.5.cloned.1.call-update
  8.7 0.7 fusion.74
  9.5 0.8 select_reduce_fusion
  10.4 1.7 fusion.46
  12.4 0.5 fusion.48
  12.8 30.0 %all-gather.3.cloned.1.call-done = bf16[3,512,512]{2,1,0:T(8,128)(2,1)} async-done(((bf16[3,128,512]{2,1,0:T(8,128)(2,1)}), bf16[3,512,512]{2,1,0:T(8,128)(2,1)}) %all-gather.3.cloned.1.call-update) | async-done | bytes 1572880 | tf_op jit(solution)/shard_map/all_gather | solution.py:32
  42.8 3.7 %fusion.54 = (bf16[512,512]{1,0:T(8,128)(2,1)S(1)}, f32[512,512]{1,0:T(8,128)}) fusion(bf16[1,512,512]{2,1,0:T(8,128)(2,1)S(1)} %copy-done.4, bf16[3,512,512]{2,1,0:T(8,128)(2,1)} %all-gather.3.cloned.1.call-done, bf16[1,512,512]{2,1,0:T(8,128)(2,1)S(1)} %get-tuple-element.8, bf16[1,512,512]{2,1,0:T(8,128)(2,1)S(1)} %fusion.48, ...), kind=kOutput, calls=%fused_computation.47 | convolution fusion | flops 810287104 | bytes 5769216 | tf_op jit(solution)/shard_map/ktd,kpd->tp/dot_general | solution.py:29
  46.7 28.8 %all-gather.5.cloned.1.call-done = bf16[3,512,512]{2,1,0:T(8,128)(2,1)} async-done(((bf16[3,128,512]{2,1,0:T(8,128)(2,1)}), bf16[3,512,512]{2,1,0:T(8,128)(2,1)}) %all-gather.5.cloned.1.call-update) | async-done | bytes 1572880 | tf_op jit(solution)/shard_map/all_gather | solution.py:32
  75.5 2.4 %fusion.42 = bf16[64,4,8,128]{3,2,1,0:T(8,128)(2,1)S(1)} fusion(f32[512,512]{1,0:T(8,128)S(1)} %copy-done.5, bf16[3,512,512]{2,1,0:T(8,128)(2,1)} %all-gather.5.cloned.1.call-done, bf16[1,512,512]{2,1,0:T(8,128)(2,1)S(1)} %get-tuple-element.6, bf16[1,512,512]{2,1,0:T(8,128)(2,1)S(1)} %bitcast.101, bf16[1,512,512]{2,1,0:T(8,128)(2,1)S(1)} %get-tuple-element.5, ...), kind=kOutput, calls=%fused_computation.36 | convolution fusion | flops 807927808 | bytes 4720640 | tf_op jit(solution)/shard_map/ktd,kpd->tp/dot_general | solution.py:29
  77.9 0.9 copy.34
  78.8 3.5 %all-to-all-start.1 = ((bf16[4,128,512]{1,2,0:T(8,128)(2,1)}), bf16[4,128,512]{1,2,0:T(8,128)(2,1)S(1)}, u32[]{:S(2)}, u32[]{:S(2)}) async-start(bf16[4,128,512]{1,2,0:T(8,128)(2,1)} %bitcast.97), calls=%async_computation.1 | async-start | bytes 1048576 | tf_op jit(solution)/shard_map/all_to_all | solution.py:47
  82.4 0.2 convolution_add_fusion
  82.6 0.7 all_to_all.30
  83.3 7.1 %all-to-all-done.1 = bf16[4,128,512]{1,2,0:T(8,128)(2,1)S(1)} async-done(((bf16[4,128,512]{1,2,0:T(8,128)(2,1)}), bf16[4,128,512]{1,2,0:T(8,128)(2,1)S(1)}, u32[]{:S(2)}, u32[]{:S(2)}) %all-to-all-start.1) | async-done | bytes 524320 | tf_op jit(solution)/shard_map/all_to_all | solution.py:47
  90.4 4.6 %all-to-all-start = ((s32[8,1,512]{2,1,0:T(1,128)}), s32[8,1,512]{2,1,0:T(1,128)S(1)}, u32[]{:S(2)}, u32[]{:S(2)}) async-start(s32[8,1,512]{2,1,0:T(1,128)} %all_to_all.30), calls=%async_computation | async-start | bytes 32768 | tf_op jit(solution)/shard_map/all_to_all | solution.py:74
  95.0 0.5 fusion.14
  95.5 1.2 copy.21
  96.7 3.9 %all-to-all-done = s32[8,1,512]{2,1,0:T(1,128)S(1)} async-done(((s32[8,1,512]{2,1,0:T(1,128)}), s32[8,1,512]{2,1,0:T(1,128)S(1)}, u32[]{:S(2)}, u32[]{:S(2)}) %all-to-all-start) | async-done | bytes 16416 | tf_op jit(solution)/shard_map/all_to_all | solution.py:74
  100.7 3.6 %all-to-all-start.2 = ((bf16[8,128,512]{1,2,0:T(8,128)(2,1)}), bf16[8,128,512]{1,2,0:T(8,128)(2,1)S(1)}, u32[]{:S(2)}, u32[]{:S(2)}) async-start(bf16[8,128,512]{1,2,0:T(8,128)(2,1)} %bitcast.25), calls=%async_computation.2 | async-start | bytes 2097152 | tf_op jit(solution)/shard_map/all_to_all | solution.py:73
  104.2 26.5 %all-to-all-done.2 = bf16[8,128,512]{1,2,0:T(8,128)(2,1)S(1)} async-done(((bf16[8,128,512]{1,2,0:T(8,128)(2,1)}), bf16[8,128,512]{1,2,0:T(8,128)(2,1)S(1)}, u32[]{:S(2)}, u32[]{:S(2)}) %all-to-all-start.2) | async-done | bytes 1048608 | tf_op jit(solution)/shard_map/all_to_all | solution.py:73
  130.9 28.2 %scatter_custom_fusion = f32[8193,128]{1,0:T(8,128)} fusion(s32[4096]{0:T(1024)S(1)} %bitcast.103, f32[4096,128]{1,0:T(8,128)S(1)} %bitcast.99, f32[]{:T(128)} %constant.8.clone.1), kind=kCustom, calls=%fused_computation.2 | custom fusion | flops 524288 | bytes 4194820 | tf_op jit(solution)/shard_map/scatter-add | solution.py:78
  159.1 4.4 %slice_bitcast_fusion = f32[128,8192]{0,1:T(8,128)} fusion(f32[8193,128]{1,0:T(8,128)} %scatter_custom_fusion), kind=kLoop, calls=%fused_computation.1 | loop fusion | bytes 8388608 | tf_op jit(solution)/shard_map/transpose | solution.py:79
  163.5 5.6 %copy.22 = f32[128,8192]{1,0:T(8,128)} copy(f32[128,8192]{0,1:T(8,128)} %slice_bitcast_fusion) | data formatting | bytes 8388608 | tf_op jit(solution)/shard_map/transpose | solution.py:79
  (24 shorter events, 0.8 us)
Async XLA Ops:
  6.5 36.2 %all-gather.3.cloned.1.call-start = ((), (), s32[]{:S(2)}) async-start(), calls=%async_computation.3 | async-start | bytes 1966080 | tf_op jit(solution)/shard_map/all_gather | solution.py:32
  7.3 68.2 %all-gather.5.cloned.1.call-start = ((), (), s32[]{:S(2)}) async-start(), calls=%async_computation.4 | async-start | bytes 1966080 | tf_op jit(solution)/shard_map/all_gather | solution.py:32
  10.3 2.0 %copy-start.2 = (s32[2048]{0:T(1024)S(1)}, s32[2048]{0:T(1024)}, u32[]{:S(2)}) copy-start(s32[2048]{0:T(1024)} %param.14) | copy-start | bytes 24580
  10.3 2.0 %copy-start = (bf16[1,512,512]{2,1,0:T(8,128)(2,1)S(1)}, bf16[1,512,512]{2,1,0:T(8,128)(2,1)}, u32[]{:S(2)}) copy-start(bf16[1,512,512]{2,1,0:T(8,128)(2,1)} %param.10) | copy-start | bytes 1572868
  10.3 2.0 %copy-start.1 = (bf16[1,512,512]{2,1,0:T(8,128)(2,1)S(1)}, bf16[1,512,512]{2,1,0:T(8,128)(2,1)}, u32[]{:S(2)}) copy-start(bf16[1,512,512]{2,1,0:T(8,128)(2,1)} %param.8) | copy-start | bytes 1572868
  12.1 30.7 %copy-start.4 = (bf16[1,512,512]{2,1,0:T(8,128)(2,1)S(1)}, bf16[1,512,512]{2,1,0:T(8,128)(2,1)}, u32[]{:S(2)}) copy-start(bf16[1,512,512]{2,1,0:T(8,128)(2,1)} %param.9) | copy-start | bytes 1572868
  46.4 29.0 %copy-start.5 = (f32[512,512]{1,0:T(8,128)S(1)}, f32[512,512]{1,0:T(8,128)}, u32[]{:S(2)}) copy-start(f32[512,512]{1,0:T(8,128)} %get-tuple-element.10) | copy-start | bytes 3145732
  77.9 4.4 %copy-start.3 = (s32[64,1]{0,1:T(1,128)S(1)}, s32[64,1]{0,1:T(1,128)}, u32[]{:S(2)}) copy-start(s32[64,1]{0,1:T(1,128)} %param.15) | copy-start | bytes 772
  78.8 11.6 %all-to-all-start.1 = ((bf16[4,128,512]{1,2,0:T(8,128)(2,1)}), bf16[4,128,512]{1,2,0:T(8,128)(2,1)S(1)}, u32[]{:S(2)}, u32[]{:S(2)}) async-start(bf16[4,128,512]{1,2,0:T(8,128)(2,1)} %bitcast.97), calls=%async_computation.1 | async-start | bytes 1048576 | tf_op jit(solution)/shard_map/all_to_all | solution.py:47
  90.4 10.3 %all-to-all-start = ((s32[8,1,512]{2,1,0:T(1,128)}), s32[8,1,512]{2,1,0:T(1,128)S(1)}, u32[]{:S(2)}, u32[]{:S(2)}) async-start(s32[8,1,512]{2,1,0:T(1,128)} %all_to_all.30), calls=%async_computation | async-start | bytes 32768 | tf_op jit(solution)/shard_map/all_to_all | solution.py:74
  100.7 30.1 %all-to-all-start.2 = ((bf16[8,128,512]{1,2,0:T(8,128)(2,1)}), bf16[8,128,512]{1,2,0:T(8,128)(2,1)S(1)}, u32[]{:S(2)}, u32[]{:S(2)}) async-start(bf16[8,128,512]{1,2,0:T(8,128)(2,1)} %bitcast.25), calls=%async_computation.2 | async-start | bytes 2097152 | tf_op jit(solution)/shard_map/all_to_all | solution.py:73
Sparse Core Ops, SparseCore 0:
  9.2 33.5 all-gather.2
  44.6 30.8 all-gather.4
where the time goes:
time: 176 us
  waiting for transfers between devices  97.7 us (56%)
  other arithmetic  32.2 us (18%)
  between operations  14.2 us (8%)
  local copies, waits for them, and re-layouts  13.4 us (8%)
  starting transfers between devices  11.7 us (7%)
  matrix products  6.8 us (4%)
    all_gather x2, waiting for transfers between devices, apply_taps(): lax.all_gather(weights, 'fsdp', axis=1, tiled=True)  58.8 us
    scatter-add x1, other arithmetic, body(): summed = jax.ops.segment_sum(flat_rows, safe_ids, num_segments=ROWS_OWN + 1)  28.2 us
    all_to_all x1, waiting for transfers between devices, body(): lax.all_to_all(send_rows, 'grp', split_axis=0, concat_axis=0, tiled=True)  26.5 us
    transpose x2, local copies, waits for them, and re-layouts, body(): return summed[:ROWS_OWN].T  10 us
    all_to_all x1, waiting for transfers between devices, body(): lax.all_to_all(row_grad.T, 'fsdp', split_axis=0, concat_axis=1, tiled=True)  7.07 us
    dot_general x2, matrix products, apply_taps(): jnp.einsum('ktd,kpd->tp', tap_rows, lax.all_gather(weights, 'fsdp', axis=...  6.08 us
    all_to_all x1, starting transfers between devices, body(): lax.all_to_all(send_ids, 'grp', split_axis=0, concat_axis=0, tiled=True)  4.6 us
    all_to_all x1, waiting for transfers between devices, body(): lax.all_to_all(send_ids, 'grp', split_axis=0, concat_axis=0, tiled=True)  3.93 us
  transfers between devices with their start and end apart: 5, of which 5 were waited for; matrix products, arithmetic and copies ran while one was open for 6% of the time, Pallas kernels for 0%

commit v1 on v0

--- a/solution.py
+++ b/solution.py
@@ -5,6 +5,22 @@
 
 BLK = 32
 ROWS_OWN = 8192
+
+
+def exchange_in_pairs(value, axis, split, join):
+    ways, here = (lax.axis_size(axis), lax.axis_index(axis))
+    width = value.shape[split] // ways
+    dims = list(value.shape)
+    dims[split] = width
+    height = dims[join]
+    dims[join] = height * ways
+    full = jnp.zeros(dims, value.dtype)
+    for mask in range(ways):
+        part = lax.dynamic_slice_in_dim(value, (here ^ mask) * width, width, axis=split)
+        if mask:
+            part = lax.ppermute(part, axis, [(d, d ^ mask) for d in range(ways)])
+        full = lax.dynamic_update_slice_in_dim(full, part, (here ^ mask) * height, axis=join)
+    return full
 
 
 def layer_back(gradient, pre_acts, live_rows, dilation, product):
@@ -71,7 +87,7 @@
     send_ids = send_ids.reshape(owner_count, slot_cap * BLK)
     recv_rows, recv_ids = (
         lax.all_to_all(send_rows, "grp", split_axis=0, concat_axis=0, tiled=True),
-        lax.all_to_all(send_ids, "grp", split_axis=0, concat_axis=0, tiled=True),
+        exchange_in_pairs(send_ids, "grp", 0, 0),
     )
     flat_rows = jnp.transpose(recv_rows, (0, 2, 1)).reshape(-1, feat_cols).astype(jnp.float32)
     safe_ids = jnp.where(recv_ids < 0, ROWS_OWN, recv_ids).reshape(-1)

time: 176 us -> 170 us (0.966)
  waiting for transfers between devices: 97.7 us -> 87.1 us
  starting transfers between devices: 11.7 us -> 16.8 us
    all_to_all x1, waiting for transfers between devices: 26.5 us -> 0.01 us  [body(): lax.all_to_all(send_rows, 'grp', split_axis=0, concat_axis=0, tiled=True)]
    ppermute x0 -> x7, waiting for transfers between devices: none -> 17.5 us  [exchange_in_pairs(): part = lax.ppermute(part, axis, [(d, d ^ mask) for d in range(ways)])]
    ppermute x0 -> x7, starting transfers between devices: none -> 8.61 us  [exchange_in_pairs(): part = lax.ppermute(part, axis, [(d, d ^ mask) for d in range(ways)])]
    all_to_all x1 -> x0, starting transfers between devices: 4.6 us -> none  [body(): lax.all_to_all(send_ids, 'grp', split_axis=0, concat_axis=0, tiled=True)]
    all_to_all x1 -> x0, waiting for transfers between devices: 3.93 us -> none  [body(): lax.all_to_all(send_ids, 'grp', split_axis=0, concat_axis=0, tiled=True)]
  transfers between devices with their start and end apart: 5 -> 11, of which waited for: 5 -> 5; matrix products, arithmetic and copies ran while one was open for 6% -> 4% of each run, Pallas kernels for 0% -> 0%
where the time goes in v1:
time: 170 us; the launch traced here: 169 us
  waiting for transfers between devices  87.1 us (51%)
  other arithmetic  30.9 us (18%)
  starting transfers between devices  16.8 us (10%)
  between operations  14.4 us (8%)
  local copies, waits for them, and re-layouts  13.3 us (8%)
  matrix products  6.8 us (4%)
    all_gather x2, waiting for transfers between devices, apply_taps(): lax.all_gather(weights, 'fsdp', axis=1, tiled=True)  60.4 us
    scatter-add x1, other arithmetic, body(): summed = jax.ops.segment_sum(flat_rows, safe_ids, num_segments=ROWS_OWN + 1)  28.2 us
    ppermute x7, waiting for transfers between devices, exchange_in_pairs(): part = lax.ppermute(part, axis, [(d, d ^ mask) for d in range(ways)])  17.5 us
    transpose x2, local copies, waits for them, and re-layouts, body(): return summed[:ROWS_OWN].T  10 us
    ppermute x7, starting transfers between devices, exchange_in_pairs(): part = lax.ppermute(part, axis, [(d, d ^ mask) for d in range(ways)])  8.61 us
    all_to_all x1, waiting for transfers between devices, body(): lax.all_to_all(row_grad.T, 'fsdp', split_axis=0, concat_axis=1, tiled=True)  7.81 us
    dot_general x2, matrix products, apply_taps(): jnp.einsum('ktd,kpd->tp', tap_rows, lax.all_gather(weights, 'fsdp', axis=...  6.08 us
    all_to_all x1, starting transfers between devices, body(): lax.all_to_all(send_rows, 'grp', split_axis=0, concat_axis=0, tiled=True)  4.73 us
  transfers between devices with their start and end apart: 11, of which 5 were waited for; matrix products, arithmetic and copies ran while one was open for 4% of the time, Pallas kernels for 0%

profile of v1, /device:TPU:0, one launch (start us, length us, event | category | flops | bytes accessed | tf_op | source)
XLA Modules:
  0.0 169.3 jit_solution(3507054277329085984)
XLA Ops:
  6.5 0.7 all-gather.3.cloned.1.call-update
  7.3 0.7 all-gather.5.cloned.1.call-update
  8.7 1.7 %fusion.46 = bf16[512,512]{1,0:T(8,128)(2,1)S(1)} fusion(bf16[1,512,512]{2,1,0:T(8,128)(2,1)} %param.8, bf16[1,512,512]{2,1,0:T(8,128)(2,1)} %param.10), kind=kLoop, calls=%fused_computation.39 | loop fusion | flops 2883584 | bytes 1572864 | tf_op jit(solution)/shard_map/convert_element_type | solution.py:30
  10.8 0.5 fusion.48
  11.2 31.6 %all-gather.3.cloned.1.call-done = bf16[3,512,512]{2,1,0:T(8,128)(2,1)} async-done(((bf16[3,128,512]{2,1,0:T(8,128)(2,1)}), bf16[3,512,512]{2,1,0:T(8,128)(2,1)}) %all-gather.3.cloned.1.call-update) | async-done | bytes 1572880 | tf_op jit(solution)/shard_map/all_gather | solution.py:48
  42.8 3.7 %fusion.54 = (bf16[512,512]{1,0:T(8,128)(2,1)S(1)}, f32[512,512]{1,0:T(8,128)}) fusion(bf16[1,512,512]{2,1,0:T(8,128)(2,1)S(1)} %copy-done.4, bf16[3,512,512]{2,1,0:T(8,128)(2,1)} %all-gather.3.cloned.1.call-done, bf16[1,512,512]{2,1,0:T(8,128)(2,1)S(1)} %get-tuple-element.8, bf16[1,512,512]{2,1,0:T(8,128)(2,1)S(1)} %fusion.48, ...), kind=kOutput, calls=%fused_computation.47 | convolution fusion | flops 810287104 | bytes 5769216 | tf_op jit(solution)/shard_map/ktd,kpd->tp/dot_general | solution.py:45
  46.7 28.8 %all-gather.5.cloned.1.call-done = bf16[3,512,512]{2,1,0:T(8,128)(2,1)} async-done(((bf16[3,128,512]{2,1,0:T(8,128)(2,1)}), bf16[3,512,512]{2,1,0:T(8,128)(2,1)}) %all-gather.5.cloned.1.call-update) | async-done | bytes 1572880 | tf_op jit(solution)/shard_map/all_gather | solution.py:48
  75.5 2.4 %fusion.42 = bf16[64,4,8,128]{3,2,1,0:T(8,128)(2,1)S(1)} fusion(f32[512,512]{1,0:T(8,128)S(1)} %copy-done.5, bf16[3,512,512]{2,1,0:T(8,128)(2,1)} %all-gather.5.cloned.1.call-done, bf16[1,512,512]{2,1,0:T(8,128)(2,1)S(1)} %get-tuple-element.6, bf16[1,512,512]{2,1,0:T(8,128)(2,1)S(1)} %bitcast.102, bf16[1,512,512]{2,1,0:T(8,128)(2,1)S(1)} %get-tuple-element.5, ...), kind=kOutput, calls=%fused_computation.36 | convolution fusion | flops 807927808 | bytes 4720640 | tf_op jit(solution)/shard_map/ktd,kpd->tp/dot_general | solution.py:45
  77.9 0.9 copy.28
  78.8 3.5 %all-to-all-start = ((bf16[4,128,512]{1,2,0:T(8,128)(2,1)}), bf16[4,128,512]{1,2,0:T(8,128)(2,1)S(1)}, u32[]{:S(2)}, u32[]{:S(2)}) async-start(bf16[4,128,512]{1,2,0:T(8,128)(2,1)} %bitcast.98), calls=%async_computation | async-start | bytes 1048576 | tf_op jit(solution)/shard_map/all_to_all | solution.py:63
  82.6 7.8 %all-to-all-done = bf16[4,128,512]{1,2,0:T(8,128)(2,1)S(1)} async-done(((bf16[4,128,512]{1,2,0:T(8,128)(2,1)}), bf16[4,128,512]{1,2,0:T(8,128)(2,1)S(1)}, u32[]{:S(2)}, u32[]{:S(2)}) %all-to-all-start) | async-done | bytes 524320 | tf_op jit(solution)/shard_map/all_to_all | solution.py:63
  90.4 0.5 fusion.14
  90.9 1.2 copy.14
  92.1 4.7 %all-to-all-start.1 = ((bf16[8,128,512]{1,2,0:T(8,128)(2,1)}), bf16[8,128,512]{1,2,0:T(8,128)(2,1)S(1)}, u32[]{:S(2)}, u32[]{:S(2)}) async-start(bf16[8,128,512]{1,2,0:T(8,128)(2,1)} %bitcast.23), calls=%async_computation.1 | async-start | bytes 2097152 | tf_op jit(solution)/shard_map/all_to_all | solution.py:89
  96.9 0.2 convolution_add_fusion
  97.3 2.1 %collective-permute-start.1 = (s32[1,512]{1,0:T(1,128)S(1)}, s32[1,512]{1,0:T(1,128)S(1)}, u32[]{:S(2)}, u32[]{:S(2)}) collective-permute-start(s32[1,512]{1,0:T(1,128)S(1)} %get-tuple-element.14), channel_id=1, source_target_pairs={{0,2},{1,3},{2,0},{3,1},{4,6},{5,7},{6,4},{7,5},{8,10},{9,11},{10,... | collective-permute-start | bytes 6152 | tf_op jit(solution)/shard_map/ppermute | solution.py:21
  99.4 2.5 %collective-permute-start.4 = (s32[1,512]{1,0:T(1,128)S(1)}, s32[1,512]{1,0:T(1,128)S(1)}, u32[]{:S(2)}, u32[]{:S(2)}) collective-permute-start(s32[1,512]{1,0:T(1,128)S(1)} %get-tuple-element.11), channel_id=1, source_target_pairs={{0,5},{1,4},{2,7},{3,6},{4,1},{5,0},{6,3},{7,2},{8,13},{9,12},{10,... | collective-permute-start | bytes 6152 | tf_op jit(solution)/shard_map/ppermute | solution.py:21
  102.1 0.4 collective-permute-start.3
  102.5 12.6 %collective-permute-done.1 = s32[1,512]{1,0:T(1,128)S(1)} collective-permute-done((s32[1,512]{1,0:T(1,128)S(1)}, s32[1,512]{1,0:T(1,128)S(1)}, u32[]{:S(2)}, u32[]{:S(2)}) %collective-permute-start.1) | collective-permute-done | bytes 2080 | tf_op jit(solution)/shard_map/ppermute | solution.py:21
  115.0 3.5 %collective-permute-start.5 = (s32[1,512]{1,0:T(1,128)S(1)}, s32[1,512]{1,0:T(1,128)S(1)}, u32[]{:S(2)}, u32[]{:S(2)}) collective-permute-start(s32[1,512]{1,0:T(1,128)S(1)} %get-tuple-element.10), channel_id=1, source_target_pairs={{0,6},{1,7},{2,4},{3,5},{4,2},{5,3},{6,0},{7,1},{8,14},{9,15},{10,... | collective-permute-start | bytes 6152 | tf_op jit(solution)/shard_map/ppermute | solution.py:21
  118.8 4.9 %collective-permute-done.3 = s32[1,512]{1,0:T(1,128)S(1)} collective-permute-done((s32[1,512]{1,0:T(1,128)S(1)}, s32[1,512]{1,0:T(1,128)S(1)}, u32[]{:S(2)}, u32[]{:S(2)}) %collective-permute-start.3) | collective-permute-done | bytes 2080 | tf_op jit(solution)/shard_map/ppermute | solution.py:21
  124.2 28.2 %scatter_custom_fusion = f32[8193,128]{1,0:T(8,128)} fusion(s32[4096]{0:T(1024)S(1)} %bitcast.103, f32[4096,128]{1,0:T(8,128)S(1)} %bitcast.100, f32[]{:T(128)} %constant.16.clone.1), kind=kCustom, calls=%fused_computation.2 | custom fusion | flops 524288 | bytes 4194820 | tf_op jit(solution)/shard_map/scatter-add | solution.py:94
  152.4 4.4 %slice_bitcast_fusion = f32[128,8192]{0,1:T(8,128)} fusion(f32[8193,128]{1,0:T(8,128)} %scatter_custom_fusion), kind=kLoop, calls=%fused_computation.1 | loop fusion | bytes 8388608 | tf_op jit(solution)/shard_map/transpose | solution.py:95
  156.9 5.6 %copy.15 = f32[128,8192]{1,0:T(8,128)} copy(f32[128,8192]{0,1:T(8,128)} %slice_bitcast_fusion) | data formatting | bytes 8388608 | tf_op jit(solution)/shard_map/transpose | solution.py:95
  (47 shorter events, 1.8 us)
Async XLA Ops:
  6.5 36.2 %all-gather.3.cloned.1.call-start = ((), (), s32[]{:S(2)}) async-start(), calls=%async_computation.2 | async-start | bytes 1966080 | tf_op jit(solution)/shard_map/all_gather | solution.py:48
  7.3 68.2 %all-gather.5.cloned.1.call-start = ((), (), s32[]{:S(2)}) async-start(), calls=%async_computation.3 | async-start | bytes 1966080 | tf_op jit(solution)/shard_map/all_gather | solution.py:48
  8.7 2.0 %copy-start.3 = (s32[64,1]{0,1:T(1,128)S(1)}, s32[64,1]{0,1:T(1,128)}, u32[]{:S(2)}) copy-start(s32[64,1]{0,1:T(1,128)} %param.15) | copy-start | bytes 772
  8.7 2.1 %copy-start = (bf16[1,512,512]{2,1,0:T(8,128)(2,1)S(1)}, bf16[1,512,512]{2,1,0:T(8,128)(2,1)}, u32[]{:S(2)}) copy-start(bf16[1,512,512]{2,1,0:T(8,128)(2,1)} %param.10) | copy-start | bytes 1572868
  8.7 2.1 %copy-start.1 = (bf16[1,512,512]{2,1,0:T(8,128)(2,1)S(1)}, bf16[1,512,512]{2,1,0:T(8,128)(2,1)}, u32[]{:S(2)}) copy-start(bf16[1,512,512]{2,1,0:T(8,128)(2,1)} %param.8) | copy-start | bytes 1572868
  10.4 32.4 %copy-start.4 = (bf16[1,512,512]{2,1,0:T(8,128)(2,1)S(1)}, bf16[1,512,512]{2,1,0:T(8,128)(2,1)}, u32[]{:S(2)}) copy-start(bf16[1,512,512]{2,1,0:T(8,128)(2,1)} %param.9) | copy-start | bytes 1572868
  46.4 29.0 %copy-start.5 = (f32[512,512]{1,0:T(8,128)S(1)}, f32[512,512]{1,0:T(8,128)}, u32[]{:S(2)}) copy-start(f32[512,512]{1,0:T(8,128)} %get-tuple-element.18) | copy-start | bytes 3145732
  78.8 11.6 %all-to-all-start = ((bf16[4,128,512]{1,2,0:T(8,128)(2,1)}), bf16[4,128,512]{1,2,0:T(8,128)(2,1)S(1)}, u32[]{:S(2)}, u32[]{:S(2)}) async-start(bf16[4,128,512]{1,2,0:T(8,128)(2,1)} %bitcast.98), calls=%async_computation | async-start | bytes 1048576 | tf_op jit(solution)/shard_map/all_to_all | solution.py:63
  92.1 4.7 %copy-start.2 = (s32[2048]{0:T(1024)S(1)}, s32[2048]{0:T(1024)}, u32[]{:S(2)}) copy-start(s32[2048]{0:T(1024)} %param.14) | copy-start | bytes 24580
  92.1 31.9 %all-to-all-start.1 = ((bf16[8,128,512]{1,2,0:T(8,128)(2,1)}), bf16[8,128,512]{1,2,0:T(8,128)(2,1)S(1)}, u32[]{:S(2)}, u32[]{:S(2)}) async-start(bf16[8,128,512]{1,2,0:T(8,128)(2,1)} %bitcast.23), calls=%async_computation.1 | async-start | bytes 2097152 | tf_op jit(solution)/shard_map/all_to_all | solution.py:89
  97.3 17.7 %collective-permute-start.1 = (s32[1,512]{1,0:T(1,128)S(1)}, s32[1,512]{1,0:T(1,128)S(1)}, u32[]{:S(2)}, u32[]{:S(2)}) collective-permute-start(s32[1,512]{1,0:T(1,128)S(1)} %get-tuple-element.14), channel_id=1, source_target_pairs={{0,2},{1,3},{2,0},{3,1},{4,6},{5,7},{6,4},{7,5},{8,10},{9,11},{10,... | collective-permute-start | bytes 6152 | tf_op jit(solution)/shard_map/ppermute | solution.py:21
  99.4 19.1 %collective-permute-start = (s32[1,512]{1,0:T(1,128)S(1)}, s32[1,512]{1,0:T(1,128)S(1)}, u32[]{:S(2)}, u32[]{:S(2)}) collective-permute-start(s32[1,512]{1,0:T(1,128)S(1)} %get-tuple-element.15), channel_id=1, source_target_pairs={{0,1},{1,0},{2,3},{3,2},{4,5},{5,4},{6,7},{7,6},{8,9},{9,8},{10,11... | collective-permute-start | bytes 6152 | tf_op jit(solution)/shard_map/ppermute | solution.py:21
  99.4 24.3 %collective-permute-start.4 = (s32[1,512]{1,0:T(1,128)S(1)}, s32[1,512]{1,0:T(1,128)S(1)}, u32[]{:S(2)}, u32[]{:S(2)}) collective-permute-start(s32[1,512]{1,0:T(1,128)S(1)} %get-tuple-element.11), channel_id=1, source_target_pairs={{0,5},{1,4},{2,7},{3,6},{4,1},{5,0},{6,3},{7,2},{8,13},{9,12},{10,... | collective-permute-start | bytes 6152 | tf_op jit(solution)/shard_map/ppermute | solution.py:21
  101.9 16.8 %collective-permute-start.2 = (s32[1,512]{1,0:T(1,128)S(1)}, s32[1,512]{1,0:T(1,128)S(1)}, u32[]{:S(2)}, u32[]{:S(2)}) collective-permute-start(s32[1,512]{1,0:T(1,128)S(1)} %get-tuple-element.13), channel_id=1, source_target_pairs={{0,3},{1,2},{2,1},{3,0},{4,7},{5,6},{6,5},{7,4},{8,11},{9,10},{10,... | collective-permute-start | bytes 6152 | tf_op jit(solution)/shard_map/ppermute | solution.py:21
  102.1 21.6 %collective-permute-start.3 = (s32[1,512]{1,0:T(1,128)S(1)}, s32[1,512]{1,0:T(1,128)S(1)}, u32[]{:S(2)}, u32[]{:S(2)}) collective-permute-start(s32[1,512]{1,0:T(1,128)S(1)} %get-tuple-element.12), channel_id=1, source_target_pairs={{0,4},{1,5},{2,6},{3,7},{4,0},{5,1},{6,2},{7,3},{8,12},{9,13},{10,... | collective-permute-start | bytes 6152 | tf_op jit(solution)/shard_map/ppermute | solution.py:21
  115.0 8.8 %collective-permute-start.5 = (s32[1,512]{1,0:T(1,128)S(1)}, s32[1,512]{1,0:T(1,128)S(1)}, u32[]{:S(2)}, u32[]{:S(2)}) collective-permute-start(s32[1,512]{1,0:T(1,128)S(1)} %get-tuple-element.10), channel_id=1, source_target_pairs={{0,6},{1,7},{2,4},{3,5},{4,2},{5,3},{6,0},{7,1},{8,14},{9,15},{10,... | collective-permute-start | bytes 6152 | tf_op jit(solution)/shard_map/ppermute | solution.py:21
  118.5 5.4 %collective-permute-start.6 = (s32[1,512]{1,0:T(1,128)S(1)}, s32[1,512]{1,0:T(1,128)S(1)}, u32[]{:S(2)}, u32[]{:S(2)}) collective-permute-start(s32[1,512]{1,0:T(1,128)S(1)} %get-tuple-element.9), channel_id=1, source_target_pairs={{0,7},{1,6},{2,5},{3,4},{4,3},{5,2},{6,1},{7,0},{8,15},{9,14},{10,... | collective-permute-start | bytes 6152 | tf_op jit(solution)/shard_map/ppermute | solution.py:21
Sparse Core Ops, SparseCore 0:
  9.2 33.5 all-gather.2
  44.6 30.8 all-gather.4
